TPU v7x, 32 devices: a whole 2x2x4 slice. The times are simulated.
32 devices in a mesh: face: 4 (over z), tile: 8 (over y, x, core).
Axes of the slice: x: 2, y: 2, z: 4, core: 2. Of those that a mesh axis runs over, the one named last changes fastest.
Arguments:
- sensitivity: float32 [8, 4, 512, 1536], P(None, None, ('face', 'tile')), may hold values from -6 to 6
- west_weight: float32 [8, 512, 1536], P(None, ('face', 'tile')), may hold values from 0.02 to 0.45
- east_weight: float32 [8, 512, 1536], P(None, ('face', 'tile')), may hold values from 0.02 to 0.45
- south_weight: float32 [8, 512, 1536], P(None, ('face', 'tile')), may hold values from 0.02 to 0.45
- north_weight: float32 [8, 512, 1536], P(None, ('face', 'tile')), may hold values from 0.02 to 0.45
- mixing_rate: float32 [7, 512, 1536], P(None, ('face', 'tile')), may hold values from 0.1 to 10
- extents: int32 [4, 8], replicated, may hold values from 1 to 16, 96 in all within a row
- rotation: int32 [4, 8], replicated, may hold values from 0 to 1
- regrid_weight: bfloat16 [3072, 256, 128], P(('face', 'tile')), may hold values from -0.375 to 0.375
- owner: int32 [3072, 1], P(('face', 'tile')), may hold values from 0 to 31; in each aligned block of 96 rows (0 to 95, 96 to 191, ...) at most 6 rows name the same one
- inv_slot: int32 [3072], P(('face', 'tile')), may hold values from 0 to 7
Outputs:
- adjoint_start: float32 [8, 4, 512, 1536], P(None, None, ('face', 'tile'))
- emission_grad: float32 [256, 4, 128], P(('face', 'tile'))
Inputs may be any that keep to these rules, and one draw needn't show every extreme that they name: The 8 extents of each face sum to 96, and the largest of each face is 16. Of the 96 blocks of one tile at most 6 name the same owner, a bound that some block reaches of them.
All inputs are finite; a program needn't handle non-finite values.
Results may differ from a plain program's by a relative error of at most 0.0029.
Values sent between devices are 32-bit elements; how exact they have to be, the bound alone decides.
A program may use at most 128 MiB of HBM per device.

v0:
```python
import jax
import jax.numpy as jnp
from jax import lax
from jax.sharding import PartitionSpec as P

NI = 8


def shifted(value, axis, steps):
    count = lax.axis_size(axis)
    pairs = [(source, (source + steps) % count) for source in range(count)]
    return lax.ppermute(value, axis, pairs)


def meridional(adjoint, south_rate, north_rate):
    south_flux = south_rate * adjoint
    north_flux = north_rate * adjoint
    edge_zero = jnp.zeros_like(adjoint[..., :1])
    return (
        (1.0 - south_rate - north_rate) * adjoint
        + jnp.concatenate([south_flux[..., 1:], edge_zero], axis=-1)
        + jnp.concatenate([edge_zero, north_flux[..., :-1]], axis=-1)
    )


def vertical_solve(rhs, rate):
    count = rhs.shape[0]
    diagonal_terms = []
    for level in range(count):
        value = 1.0 + jnp.zeros_like(rate[0])
        if level > 0:
            value = value + rate[level - 1]
        if level < count - 1:
            value = value + rate[level]
        diagonal_terms.append(value)
    pivot = diagonal_terms[0]
    upper_part = [-rate[0] / pivot]
    solved = [rhs[0] / pivot]
    for level in range(1, count):
        pivot = diagonal_terms[level] + rate[level - 1] * upper_part[-1]
        if level < count - 1:
            upper_part.append(-rate[level] / pivot)
        solved.append((rhs[level] + rate[level - 1] * solved[-1]) / pivot)
    result = [solved[-1]]
    for level in range(count - 2, -1, -1):
        result.insert(0, solved[level] - upper_part[level] * result[0])
    return jnp.stack(result)


def per_device(
    sensitivity,
    west_weight,
    east_weight,
    south_weight,
    north_weight,
    mixing_rate,
    extents,
    rotation,
    regrid_weight,
    owner,
    inv_slot,
):
    levels, species, tile_rows, width = sensitivity.shape
    block_count, block_cells, inv_cells = regrid_weight.shape
    device_count = lax.axis_size(("face", "tile"))
    position = lax.axis_index(("face", "tile"))
    ext_all = extents.reshape(-1)
    rot_all = rotation.reshape(-1)
    my_extent = ext_all[position]
    my_rotation = rot_all[position]
    next_rotation = rot_all[(position + 1) % device_count]
    row_ids = jnp.arange(tile_rows, dtype=jnp.int32)
    live_rows = (row_ids < my_extent).astype(jnp.float32)[:, None]
    first_pick = (row_ids == 0).astype(jnp.float32)[:, None]
    last_pick = (row_ids == my_extent - 1).astype(jnp.float32)[:, None]
    adjoint = sensitivity * live_rows
    west_rate = west_weight[:, None]
    east_rate = east_weight[:, None]
    west_flux = west_rate * adjoint
    east_flux = east_rate * adjoint
    east_edge = jnp.sum(east_flux * last_pick, axis=2)
    west_edge = west_flux[:, :, 0, :]
    from_west = shifted(east_edge, ("face", "tile"), 1)
    from_east = shifted(west_edge, ("face", "tile"), -1)
    from_west = jnp.where(my_rotation == 1, jnp.flip(from_west, -1), from_west)
    from_east = jnp.where(next_rotation == 1, jnp.flip(from_east, -1), from_east)
    zero_row = jnp.zeros_like(adjoint[:, :, :1])
    moved = (
        (1.0 - west_rate - east_rate) * adjoint
        + jnp.concatenate([west_flux[:, :, 1:], zero_row], axis=2)
        + jnp.concatenate([zero_row, east_flux[:, :, :-1]], axis=2)
    )
    moved = (
        moved + first_pick * from_west[:, :, None] + last_pick * from_east[:, :, None]
    ) * live_rows
    moved = meridional(moved, south_weight[:, None], north_weight[:, None])
    adjoint_start = vertical_solve(moved, mixing_rate[:, None])
    surface = adjoint_start[0].astype(jnp.bfloat16).reshape(species, block_count, block_cells)
    terms = jnp.einsum("snr,nre->nse", surface, regrid_weight, preferred_element_type=jnp.float32)
    flat_terms = terms.reshape(block_count, species * inv_cells)
    owner_ids = owner[:, 0]
    target = owner_ids * NI + inv_slot
    columns = jnp.arange(NI * lax.axis_size(("face", "tile")), dtype=jnp.int32)
    select = (target[:, None] == columns[None, :]).astype(jnp.float32)
    grad = lax.psum_scatter(
        jnp.dot(
            select.T,
            flat_terms,
            precision=lax.Precision.HIGHEST,
            preferred_element_type=jnp.float32,
        ),
        ("face", "tile"),
        scatter_dimension=0,
        tiled=True,
    )
    return (adjoint_start, grad.reshape(NI, species, inv_cells))


def solution(mesh):
    placed = (
        P(None, None, ("face", "tile"), None),
        P(None, ("face", "tile"), None),
        P(None, ("face", "tile"), None),
        P(None, ("face", "tile"), None),
        P(None, ("face", "tile"), None),
        P(None, ("face", "tile"), None),
        P(),
        P(),
        P(("face", "tile"), None, None),
        P(("face", "tile"), None),
        P(("face", "tile")),
    )
    return jax.shard_map(
        per_device,
        mesh=mesh,
        in_specs=placed,
        out_specs=(P(None, None, ("face", "tile"), None), P(("face", "tile"), None, None)),
        check_vma=False,
    )
```

profile of v0, /device:TPU:0, one launch (start us, length us, event | category | flops | bytes accessed | tf_op | source)
XLA Modules:
  0.0 268.8 jit_solution(13191930593314260551)
XLA Ops:
  10.0 1.6 copy.25
  11.6 1.6 copy.26
  13.2 4.9 %multiply_reduce_fusion = (f32[8,4,1536]{2,0,1:T(8,128)}, f32[8,4,16,1536]{3,0,2,1:T(8,128)}, f32[8,4,16,1536]{3,0,2,1:T(8,128)S(1)}) fusion(f32[16]{0:T(128)S(1)} %get-tuple-element.80, f32[16]{0:T(128)S(1)} %get-tuple-element.81, f32[8,4,16,1536]{3,2,1,0:T(8,128)S(1)} %copy-done, f32[8,16,1536]{2,0,1:T(8,128)S(1)} %copy.26, f32[8,16,1536]{2,0,1:T(8,128)S(1)} %copy.25), kind=kLoop, calls=%fused_computation.5 | loop fusion | flops 3883008 | bytes 11206784 | tf_op jit(solution)/shard_map/reduce_sum | solution.py:81
  20.6 6.4 %collective-permute-start.1 = (f32[8,4,1536]{2,0,1:T(8,128)}, f32[8,4,1536]{2,0,1:T(8,128)}, u32[]{:S(2)}, u32[]{:S(2)}) collective-permute-start(f32[8,4,1536]{2,0,1:T(8,128)} %slice_bitcast_fusion), channel_id=1, source_target_pairs={{0,31},{1,0},{2,1},{3,2},{4,3},{5,4},{6,5},{7,6},{8,7},{9,8},{10,9... | collective-permute-start | bytes 589832 | tf_op jit(solution)/shard_map/ppermute | solution.py:12
  26.9 3.8 %slice.115 = f32[8,4,15,1536]{3,0,2,1:T(8,128)} slice(f32[8,4,16,1536]{3,0,2,1:T(8,128)} %copy-done.1), slice={[0:8], [0:4], [1:16], [0:1536]} | slice | bytes 5898240 | tf_op jit(solution)/shard_map/slice | solution.py:90
  32.2 1.3 broadcast_add_fusion
  36.4 3.8 %slice.116 = f32[8,4,15,1536]{3,0,2,1:T(8,128)} slice(f32[8,4,16,1536]{3,0,2,1:T(8,128)} %get-tuple-element.43), slice={[0:8], [0:4], [0:15], [0:1536]} | slice | bytes 5898240 | tf_op jit(solution)/shard_map/slice | solution.py:91
  40.2 1.3 copy.23
  41.8 1.3 copy.98
  43.3 1.3 copy.97
  44.6 1.4 copy.22
  46.1 1.5 div.255
  47.6 1.5 div.258
  49.1 1.5 div.261
  50.7 1.5 div.264
  52.2 1.5 div.267
  53.8 1.5 div.270
  56.0 1.5 mul.529
  57.5 1.5 mul.534
  59.1 1.5 mul.539
  62.6 1.5 div.252
  64.1 1.5 mul.524
  65.7 1.5 mul.546
  67.2 1.5 mul.526
  68.8 1.5 mul.531
  70.3 1.5 mul.536
  71.9 1.5 mul.541
  73.4 1.6 mul.551
  75.0 1.5 mul.556
  77.2 5.0 %rev.7 = f32[8,4,1536]{2,0,1:T(8,128)S(1)} reverse(f32[8,4,1536]{2,0,1:T(8,128)} %collective-permute-done), dimensions={2} | reverse | bytes 393216 | tf_op jit(solution)/shard_map/jit(_flip)/rev | solution.py:85
  82.2 4.8 %rev.8 = f32[8,4,1536]{2,0,1:T(8,128)S(1)} reverse(f32[8,4,1536]{2,0,1:T(8,128)} %collective-permute-done.1), dimensions={2} | reverse | bytes 393216 | tf_op jit(solution)/shard_map/jit(_flip)/rev | solution.py:86
  88.0 6.4 %add_multiply_fusion = f32[8,4,16,1536]{3,0,2,1:T(8,128)S(1)} fusion(f32[8,4,15,1536]{3,0,2,1:T(8,128)} %slice.116, f32[8,4,15,1536]{3,0,2,1:T(8,128)} %slice.115, f32[8,4,16,1536]{3,2,1,0:T(8,128)S(1)} %copy-done, f32[8,4,1536]{2,0,1:T(8,128)S(1)} %broadcast_select_fusion, f32[8,4,1536]{2,0,1:T(8,128)S(1)} %broadcast_select_fusion.1, ...), kind=kLoop, calls=%fused_computation.4 | loop fusion | flops 7077888 | bytes 13369536 | tf_op jit(solution)/shard_map/mul | solution.py:93
  95.6 1.4 pad_add_fusion
  97.0 9.7 %slice_reduce_fusion.7 = (f32[4,16,1536]{2,1,0:T(8,128)}, f32[4,16,1536]{2,1,0:T(8,128)}, f32[4,16,1536]{2,1,0:T(8,128)}, f32[4,16,1536]{2,1,0:T(8,128)}, f32[4,...) fusion(f32[8,4,16,1536]{3,0,2,1:T(8,128)S(1)} %pad_add_fusion), kind=kLoop, calls=%fused_computation.47 | loop fusion | bytes 6291456 | tf_op jit(solution)/shard_map/slice | solution.py:38
  106.7 1.8 squeeze.22
  108.6 1.8 squeeze.23
  110.4 1.8 squeeze.24
  112.2 1.8 squeeze.25
  114.0 1.8 squeeze.26
  115.9 1.8 squeeze.27
  117.7 1.8 squeeze.28
  120.4 7.6 %fusion.9 = f32[96,4,128]{2,1,0:T(4,128)S(1)} fusion(bf16[96,256,128]{2,1,0:T(8,128)(2,1)} %param.19, f32[4,96,256]{2,1,0:T(8,128)} %squeeze.29, f32[4,96,256]{2,1,0:T(8,128)} %squeeze.28, f32[4,96,256]{2,1,0:T(8,128)} %squeeze.27, f32[4,96,256]{2,1,0:T(8,128)} %squeeze.26, f32[4,96,256]{2,1,0:T(8,128)} %squeeze.25, f32[4,96,256]{2,1,0:T(8,128)} %squeeze.24, ...), kind=kOutput, calls=%fused_computation.49 | convolution fusion | flops 28803072 | bytes 11796480 | tf_op jit(solution)/shard_map/snr,nre->nse/dot_general | solution.py:99
  129.4 4.5 %add_divide_fusion.1 = (f32[1,4,16,1536]{3,0,2,1:T(1,128)S(1)}, f32[1,4,16,1536]{3,0,2,1:T(1,128)S(1)}, f32[1,4,16,1536]{3,0,2,1:T(1,128)S(1)}, f32[1,4,16,1536]...) fusion(f32[8,4,16,1536]{3,0,2,1:T(8,128)S(1)} %pad_add_fusion, ...), kind=kLoop, calls=%fused_computation.34 | loop fusion | flops 1867776 | bytes 6782976 | tf_op jit(solution)/shard_map/div | solution.py:43
  134.0 3.9 %multiply_subtract_fusion = (f32[1,4,16,1536]{3,0,2,1:T(1,128)S(1)}, f32[1,4,16,1536]{3,0,2,1:T(1,128)}, f32[1,4,16,1536]{3,0,2,1:T(1,128)}, f32[1,4,16,1536]{3,...) fusion(f32[1,4,16,1536]{3,0,2,1:T(1,128)S(1)} %get-tuple-elemen, ...), kind=kLoop, calls=%fused_computation.26 | loop fusion | flops 1671168 | bytes 7176192 | tf_op jit(solution)/shard_map/sub | solution.py:46
  138.0 7.9 %stack.2 = f32[8,4,16,1536]{3,0,2,1:T(8,128)S(1)} concatenate(f32[1,4,16,1536]{3,0,2,1:T(1,128)S(1)} %get-tuple-element.14, f32[1,4,16,1536]{3,0,2,1:T(1,128)} %get-tuple-element.15, f32[1,4,16,1536]{3,0,2,1:T(1,128)} %get-tuple-element.16, f32[1,4,16,1536]{3,0,2,1:T(1,128)} %get-tuple-element.17, f32[1,4,16,1536]{3,0,2,1:T(1,128)} %get-tuple-element.18, ...), dimensions={0} | concatenate | bytes 6291456 | tf_op jit(solution)/shard_map/stack | solution.py:47
  145.9 3.5 %copy.37 = f32[8,4,16,1536]{3,2,1,0:T(8,128)} copy(f32[8,4,16,1536]{3,0,2,1:T(8,128)S(1)} %stack.2) | data formatting | bytes 6291456
  149.4 111.2 %reduce-scatter.2.cloned.1.call-done = f32[8,512]{1,0:T(8,128)} async-done(((f32[256,512]{1,0:T(8,128)}), f32[8,512]{1,0:T(8,128)}) %reduce-scatter.2.cloned.1.call-update) | async-done | bytes 16400 | tf_op jit(solution)/shard_map/reduce_scatter | solution.py:105
  260.6 1.3 copy.38
  (86 shorter events, 15.7 us)
Async XLA Ops:
  7.2 6.1 %copy-start = (f32[8,4,16,1536]{3,2,1,0:T(8,128)S(1)}, f32[8,4,16,1536]{3,2,1,0:T(8,128)}, u32[]{:S(2)}) copy-start(f32[8,4,16,1536]{3,2,1,0:T(8,128)} %param.11) | copy-start | bytes 9437188
  7.2 253.4 %reduce-scatter.2.cloned.1.call-start = ((), (), s32[]{:S(2)}) async-start(), calls=%async_computation.1 | async-start | bytes 540672 | tf_op jit(solution)/shard_map/reduce_scatter | solution.py:105
  18.2 1.7 copy-start.1
  18.2 59.0 %collective-permute-start = (f32[8,4,1536]{2,0,1:T(8,128)}, f32[8,4,1536]{2,0,1:T(8,128)}, u32[]{:S(2)}, u32[]{:S(2)}) collective-permute-start(f32[8,4,1536]{2,0,1:T(8,128)} %get-tuple-element.42), channel_id=1, source_target_pairs={{0,1},{1,2},{2,3},{3,4},{4,5},{5,6},{6,7},{7,8},{8,9},{9,10},{10,1... | collective-permute-start | bytes 589832 | tf_op jit(solution)/shard_map/ppermute | solution.py:12
  20.6 61.6 %collective-permute-start.1 = (f32[8,4,1536]{2,0,1:T(8,128)}, f32[8,4,1536]{2,0,1:T(8,128)}, u32[]{:S(2)}, u32[]{:S(2)}) collective-permute-start(f32[8,4,1536]{2,0,1:T(8,128)} %slice_bitcast_fusion), channel_id=1, source_target_pairs={{0,31},{1,0},{2,1},{3,2},{4,3},{5,4},{6,5},{7,6},{8,7},{9,8},{10,9... | collective-permute-start | bytes 589832 | tf_op jit(solution)/shard_map/ppermute | solution.py:12
  26.9 3.8 %copy-start.5 = (f32[8,16,1536]{2,1,0:T(8,128)S(1)}, f32[8,16,1536]{2,1,0:T(8,128)}, u32[]{:S(2)}) copy-start(f32[8,16,1536]{2,1,0:T(8,128)} %param.13) | copy-start | bytes 2359300
  26.9 3.8 %copy-start.6 = (f32[8,16,1536]{2,1,0:T(8,128)S(1)}, f32[8,16,1536]{2,1,0:T(8,128)}, u32[]{:S(2)}) copy-start(f32[8,16,1536]{2,1,0:T(8,128)} %param.12) | copy-start | bytes 2359300
  26.9 5.3 %copy-start.10 = (f32[7,16,1536]{2,1,0:T(8,128)S(1)}, f32[7,16,1536]{2,1,0:T(8,128)}, u32[]{:S(2)}) copy-start(f32[7,16,1536]{2,1,0:T(8,128)} %param.16) | copy-start | bytes 2064388
  30.7 3.7 %copy-start.28 = (s32[4,8]{1,0:T(4,128)S(1)}, s32[4,8]{1,0:T(4,128)}, u32[]{:S(2)}) copy-start(s32[4,8]{1,0:T(4,128)} %param.18) | copy-start | bytes 388
  33.5 21.8 %copy-start.11 = (f32[1,16,1536]{2,1,0:T(8,128)}, f32[1,16,1536]{2,1,0:T(8,128)S(1)}, u32[]{:S(2)}) copy-start(f32[1,16,1536]{2,1,0:T(8,128)S(1)} %get-tuple-element.58) | copy-start | bytes 294916
  33.5 27.1 %copy-start.17 = (f32[1,16,1536]{2,1,0:T(8,128)}, f32[1,16,1536]{2,1,0:T(8,128)S(1)}, u32[]{:S(2)}) copy-start(f32[1,16,1536]{2,1,0:T(8,128)S(1)} %get-tuple-element.63) | copy-start | bytes 294916
  33.6 27.7 %copy-start.15 = (f32[1,16,1536]{2,1,0:T(8,128)}, f32[1,16,1536]{2,1,0:T(8,128)S(1)}, u32[]{:S(2)}) copy-start(f32[1,16,1536]{2,1,0:T(8,128)S(1)} %get-tuple-element.61) | copy-start | bytes 294916
  33.6 28.4 %copy-start.13 = (f32[1,16,1536]{2,1,0:T(8,128)}, f32[1,16,1536]{2,1,0:T(8,128)S(1)}, u32[]{:S(2)}) copy-start(f32[1,16,1536]{2,1,0:T(8,128)S(1)} %get-tuple-element.59) | copy-start | bytes 294916
  34.5 5.7 %copy-start.9 = (f32[8,16,1536]{2,1,0:T(8,128)S(1)}, f32[8,16,1536]{2,1,0:T(8,128)}, u32[]{:S(2)}) copy-start(f32[8,16,1536]{2,1,0:T(8,128)} %subtract_subtract_fusion) | copy-start | bytes 2359300
  36.4 5.1 %copy-start.7 = (f32[8,16,1536]{2,1,0:T(8,128)S(1)}, f32[8,16,1536]{2,1,0:T(8,128)}, u32[]{:S(2)}) copy-start(f32[8,16,1536]{2,1,0:T(8,128)} %param.14) | copy-start | bytes 2359300
  40.2 3.0 %copy-start.8 = (f32[8,16,1536]{2,1,0:T(8,128)S(1)}, f32[8,16,1536]{2,1,0:T(8,128)}, u32[]{:S(2)}) copy-start(f32[8,16,1536]{2,1,0:T(8,128)} %param.15) | copy-start | bytes 2359300
  46.1 41.9 %copy-start.29 = (f32[16]{0:T(128)S(1)}, f32[16]{0:T(128)}, u32[]{:S(2)}) copy-start(f32[16]{0:T(128)} %compare_convert_fusion.1) | copy-start | bytes 196
  88.0 6.4 %copy-start.2 = (f32[8,16,1535]{2,0,1:T(8,128)S(1)}, f32[8,16,1535]{2,0,1:T(8,128)}, u32[]{:S(2)}) copy-start(f32[8,16,1535]{2,0,1:T(8,128)} %copy.98) | copy-start | bytes 2357764
  88.0 6.4 %copy-start.4 = (f32[8,16,1535]{2,0,1:T(8,128)S(1)}, f32[8,16,1535]{2,0,1:T(8,128)}, u32[]{:S(2)}) copy-start(f32[8,16,1535]{2,0,1:T(8,128)} %copy.97) | copy-start | bytes 2357764
  94.4 1.2 copy-start.3
  120.4 8.9 %copy-start.22 = (f32[1,16,1536]{2,1,0:T(8,128)S(1)}, f32[1,16,1536]{2,1,0:T(8,128)}, u32[]{:S(2)}) copy-start(f32[1,16,1536]{2,1,0:T(8,128)} %get-tuple-element.60) | copy-start | bytes 294916
  120.4 8.9 %copy-start.23 = (f32[1,16,1536]{2,1,0:T(8,128)S(1)}, f32[1,16,1536]{2,1,0:T(8,128)}, u32[]{:S(2)}) copy-start(f32[1,16,1536]{2,1,0:T(8,128)} %get-tuple-element.62) | copy-start | bytes 294916
  120.4 9.0 %copy-start.24 = (f32[1,16,1536]{2,1,0:T(8,128)S(1)}, f32[1,16,1536]{2,1,0:T(8,128)}, u32[]{:S(2)}) copy-start(f32[1,16,1536]{2,1,0:T(8,128)} %get-tuple-element.64) | copy-start | bytes 294916
  120.4 9.0 %copy-start.25 = (f32[1,16,1536]{2,1,0:T(8,128)S(1)}, f32[1,16,1536]{2,1,0:T(8,128)}, u32[]{:S(2)}) copy-start(f32[1,16,1536]{2,1,0:T(8,128)} %get-tuple-element.66) | copy-start | bytes 294916
  129.3 4.6 %copy-start.12 = (f32[1,16,1536]{2,1,0:T(8,128)S(1)}, f32[1,16,1536]{2,1,0:T(8,128)}, u32[]{:S(2)}) copy-start(f32[1,16,1536]{2,1,0:T(8,128)} %copy-done.11) | copy-start | bytes 294916
  129.3 4.6 %copy-start.14 = (f32[1,16,1536]{2,1,0:T(8,128)S(1)}, f32[1,16,1536]{2,1,0:T(8,128)}, u32[]{:S(2)}) copy-start(f32[1,16,1536]{2,1,0:T(8,128)} %copy-done.13) | copy-start | bytes 294916
  129.4 4.6 %copy-start.16 = (f32[1,16,1536]{2,1,0:T(8,128)S(1)}, f32[1,16,1536]{2,1,0:T(8,128)}, u32[]{:S(2)}) copy-start(f32[1,16,1536]{2,1,0:T(8,128)} %copy-done.15) | copy-start | bytes 294916
  129.4 4.6 %copy-start.18 = (f32[1,16,1536]{2,1,0:T(8,128)S(1)}, f32[1,16,1536]{2,1,0:T(8,128)}, u32[]{:S(2)}) copy-start(f32[1,16,1536]{2,1,0:T(8,128)} %copy-done.17) | copy-start | bytes 294916
  129.4 4.6 %copy-start.19 = (f32[1,16,1536]{2,1,0:T(8,128)S(1)}, f32[1,16,1536]{2,1,0:T(8,128)}, u32[]{:S(2)}) copy-start(f32[1,16,1536]{2,1,0:T(8,128)} %get-tuple-element.65) | copy-start | bytes 294916
  129.4 4.6 %copy-start.20 = (f32[1,16,1536]{2,1,0:T(8,128)S(1)}, f32[1,16,1536]{2,1,0:T(8,128)}, u32[]{:S(2)}) copy-start(f32[1,16,1536]{2,1,0:T(8,128)} %get-tuple-element.67) | copy-start | bytes 294916
  129.4 4.6 %copy-start.21 = (f32[1,16,1536]{2,1,0:T(8,128)S(1)}, f32[1,16,1536]{2,1,0:T(8,128)}, u32[]{:S(2)}) copy-start(f32[1,16,1536]{2,1,0:T(8,128)} %get-tuple-element.69) | copy-start | bytes 294916
  129.4 4.6 %copy-start.26 = (f32[16,1536]{1,0:T(8,128)S(1)}, f32[16,1536]{1,0:T(8,128)}, u32[]{:S(2)}) copy-start(f32[16,1536]{1,0:T(8,128)} %get-tuple-element.56) | copy-start | bytes 294916
  129.4 4.6 %copy-start.27 = (f32[16,1536]{1,0:T(8,128)S(1)}, f32[16,1536]{1,0:T(8,128)}, u32[]{:S(2)}) copy-start(f32[16,1536]{1,0:T(8,128)} %get-tuple-element.57) | copy-start | bytes 294916
Sparse Core Ops, SparseCore 0:
  129.4 131.1 reduce-scatter.1
where the time goes:
time: 271 us; the launch traced here: 269 us
  waiting for transfers between devices  111 us (41%)
  local copies, waits for them, and re-layouts  97.9 us (36%)
  other arithmetic  27.5 us (10%)
  between operations  16.3 us (6%)
  matrix products  8.9 us (3%)
  starting transfers between devices  6.86 us (3%)
    reduce_scatter x1, waiting for transfers between devices, per_device(): lax.psum_scatter(jnp.dot(select.T, flat_terms, precision=lax.Precision.HI...  111 us
    unnamed x66, local copies, waits for them, and re-layouts  12.1 us
    squeeze x7, local copies, waits for them, and re-layouts, vertical_solve(): solved.append((rhs[level] + rate[level - 1] * solved[-1]) / pivot)  11.8 us
    mul x7, local copies, waits for them, and re-layouts, vertical_solve(): solved.append((rhs[level] + rate[level - 1] * solved[-1]) / pivot)  10.8 us
    div x7, local copies, waits for them, and re-layouts, vertical_solve(): solved.append((rhs[level] + rate[level - 1] * solved[-1]) / pivot)  9.93 us
    slice x1, local copies, waits for them, and re-layouts, vertical_solve(): solved = [rhs[0] / pivot]  9.72 us
    mul x7, local copies, waits for them, and re-layouts, vertical_solve(): result.insert(0, solved[level] - upper_part[level] * result[0])  8.14 us
    another operation x1, local copies, waits for them, and re-layouts, vertical_solve(): return jnp.stack(result)  7.92 us
  transfers between devices with their start and end apart: 3, of which 1 were waited for; matrix products, arithmetic and copies ran while one was open for 28% of the time, Pallas kernels for 0%

commit v1 on v0

v1 whole, which is shorter than its diff:
```python
import functools

import jax
import jax.numpy as jnp
from jax import lax
from jax.experimental import pallas as pl
from jax.experimental.pallas import tpu as pltpu
from jax.sharding import PartitionSpec as P

NI = 8
LANES = 128
MESH = pl.DeviceIdType.MESH


def edge_kernel(faces, tiles, ext_ref, sens_hbm, west_hbm, east_hbm, from_west, from_east,
                sens_v, west_v, east_v, east_edge, west_edge, load_sem, send_sem, recv_sem):
    levels, species = sens_v.shape[:2]
    face, tile = lax.axis_index("face"), lax.axis_index("tile")
    count = faces * tiles
    position = face * tiles + tile
    after, before = lax.rem(position + 1, count), lax.rem(position + count - 1, count)
    after = (after // tiles, lax.rem(after, tiles))
    before = (before // tiles, lax.rem(before, tiles))
    barrier = pltpu.get_barrier_semaphore()
    for other in (after, before):
        pl.semaphore_signal(barrier, inc=1, device_id=other, device_id_type=MESH)
    loads = [
        pltpu.make_async_copy(source, sink, load_sem.at[number])
        for number, (source, sink) in enumerate(
            ((sens_hbm, sens_v), (west_hbm, west_v), (east_hbm, east_v))
        )
    ]
    for load in loads:
        load.start()
    for load in loads:
        load.wait()
    last = ext_ref[face, tile] - 1
    picked = lax.broadcasted_iota(jnp.int32, sens_v.shape[2:], 0) == last
    for level in range(levels):
        east_rows = jnp.where(picked, east_v[level], 0.0)
        for kind in range(species):
            row = level * species + kind
            east_edge[row:row + 1, :] = jnp.sum(
                east_rows * sens_v[level, kind], axis=0, keepdims=True)
    pl.semaphore_wait(barrier, 2)
    forward = pltpu.make_async_remote_copy(
        src_ref=east_edge, dst_ref=from_west, send_sem=send_sem.at[0], recv_sem=recv_sem.at[0],
        device_id=after, device_id_type=MESH)
    forward.start()
    for level in range(levels):
        west_row = west_v[level, 0:1, :]
        for kind in range(species):
            row = level * species + kind
            west_edge[row:row + 1, :] = west_row * sens_v[level, kind, 0:1, :]
    backward = pltpu.make_async_remote_copy(
        src_ref=west_edge, dst_ref=from_east, send_sem=send_sem.at[1], recv_sem=recv_sem.at[1],
        device_id=before, device_id_type=MESH)
    backward.start()
    forward.wait()
    backward.wait()


def tile_kernel(faces, tiles, ext_ref, rot_ref, sens_hbm, west_hbm, east_hbm, south_hbm, north_hbm,
                rate_hbm, regrid_hbm, fw_hbm, fe_hbm, target_ref, out_hbm, part_ref,
                sens_v, west_v, east_v, south_v, north_v, rate_v, regrid_v, fw_v, fe_v, fw_k, fe_k,
                solved, upper, flat, terms, level_sem, rate_sem, regrid_sem, edge_sem, out_sem):
    levels, species, rows, width = sens_v.shape
    chunks = width // LANES
    blocks, cells, inv_cells = regrid_v.shape
    per_row = width // cells
    face, tile = lax.axis_index("face"), lax.axis_index("tile")
    count = faces * tiles
    after = lax.rem(face * tiles + tile + 1, count)
    extent = ext_ref[face, tile]
    my_rotation = rot_ref[face, tile]
    next_rotation = rot_ref[after // tiles, lax.rem(after, tiles)]

    edges = [
        pltpu.make_async_copy(fw_hbm, fw_v, edge_sem.at[0]),
        pltpu.make_async_copy(fe_hbm, fe_v, edge_sem.at[1]),
    ]
    rates = pltpu.make_async_copy(rate_hbm, rate_v.at[pl.ds(1, levels - 1)], rate_sem)
    regrid = pltpu.make_async_copy(regrid_hbm, regrid_v, regrid_sem)

    def level_copies(level):
        pairs = ((sens_hbm, sens_v), (west_hbm, west_v), (east_hbm, east_v),
                 (south_hbm, south_v), (north_hbm, north_v))
        return [
            pltpu.make_async_copy(source.at[level], sink.at[level], level_sem.at[number, level])
            for number, (source, sink) in enumerate(pairs)
        ]

    for edge in edges:
        edge.start()
    for copy in level_copies(0):
        copy.start()
    rates.start()
    for level in range(1, levels):
        for copy in level_copies(level):
            copy.start()
    regrid.start()

    zero_field = jnp.zeros((rows, width), jnp.float32)
    upper[0] = zero_field
    for kind in range(species):
        solved[0, kind] = zero_field
    flat[...] = jnp.zeros_like(flat)
    for edge in edges:
        edge.wait()

    def flip(ref):
        back = (lax.broadcasted_iota(jnp.int32, (LANES, LANES), 0)
                + lax.broadcasted_iota(jnp.int32, (LANES, LANES), 1) == LANES - 1).astype(jnp.float32)
        value = [
            jnp.dot(ref[:, c * LANES:(c + 1) * LANES], back, precision=lax.Precision.HIGHEST,
                    preferred_element_type=jnp.float32)
            for c in range(chunks)
        ]
        for c in range(chunks):
            ref[:, c * LANES:(c + 1) * LANES] = value[chunks - 1 - c]

    @pl.when(my_rotation == 1)
    def _():
        flip(fw_v)

    @pl.when(next_rotation == 1)
    def _():
        flip(fe_v)

    for source, sink in ((fw_v, fw_k), (fe_v, fe_k)):
        for level in range(levels):
            sink[level] = source[level * species:(level + 1) * species, :]
    rates.wait()
    rate_v[0] = zero_field
    rate_v[levels] = zero_field
    row_ids = lax.broadcasted_iota(jnp.int32, (rows, LANES), 0)
    lane_ids = lax.broadcasted_iota(jnp.int32, (rows, LANES), 1)
    live = row_ids < extent
    first, last = row_ids == 0, row_ids == extent - 1
    lane_first, lane_last = lane_ids == 0, lane_ids == LANES - 1
    zero = jnp.zeros((rows, LANES), jnp.float32)

    def forward(level, carry):
        for copy in level_copies(level):
            copy.wait()
        held = None
        before = [zero] * species
        for c in range(chunks + 1):
            fresh = [(None, zero, zero)] * species
            if c < chunks:
                cols = slice(c * LANES, (c + 1) * LANES)
                west, east = west_v[level, :, cols], east_v[level, :, cols]
                south, north = south_v[level, :, cols], north_v[level, :, cols]
                keep_x = 1.0 - west - east
                keep_y = 1.0 - south - north
                fresh = []
                for kind in range(species):
                    adjoint = jnp.where(live, sens_v[level, kind, :, cols], 0.0)
                    up = jnp.where(last, fe_k[level, kind:kind + 1, cols], pltpu.roll(west * adjoint, rows - 1, 0))
                    down = jnp.where(first, fw_k[level, kind:kind + 1, cols], pltpu.roll(east * adjoint, 1, 0))
                    moved = jnp.where(live, keep_x * adjoint + up + down, 0.0)
                    fresh.append((
                        keep_y * moved,
                        pltpu.roll(south * moved, LANES - 1, 1),
                        pltpu.roll(north * moved, 1, 1),
                    ))
            if c > 0:
                cols = slice((c - 1) * LANES, c * LANES)
                low, high = rate_v[level, :, cols], rate_v[level + 1, :, cols]
                pivot = (1.0 + low + high) + low * upper[level, :, cols]
                inverse = 1.0 / pivot
                upper[level + 1, :, cols] = -high * inverse
                for kind in range(species):
                    centre, left, right = held[kind]
                    y_adjoint = (centre + jnp.where(lane_last, fresh[kind][1], left)
                                 + jnp.where(lane_first, before[kind], right))
                    solved[level + 1, kind, :, cols] = (
                        y_adjoint + low * solved[level, kind, :, cols]) * inverse
                before = [held[kind][2] for kind in range(species)]
            held = fresh
        return carry

    lax.fori_loop(0, levels, forward, 0)

    def out_copy(level):
        return pltpu.make_async_copy(solved.at[level + 1], out_hbm.at[level], out_sem.at[level])

    out_copy(levels - 1).start()

    def backward(step, carry):
        level = levels - 2 - step
        for c in range(chunks):
            cols = slice(c * LANES, (c + 1) * LANES)
            factor = upper[level + 1, :, cols]
            for kind in range(species):
                solved[level + 1, kind, :, cols] = (
                    solved[level + 1, kind, :, cols] - factor * solved[level + 2, kind, :, cols])
        out_copy(level).start()
        return carry

    lax.fori_loop(0, levels - 1, backward, 0)

    for c in range(chunks):
        for kind in range(species):
            flat[c, pl.ds(kind, rows, stride=8), :] = solved[1, kind, :, c * LANES:(c + 1) * LANES]
    regrid.wait()
    lane_parts = cells // LANES

    def regrid_row(row, carry):
        for part in range(per_row):
            surface = jnp.concatenate(
                [flat[part * lane_parts + p, pl.ds(pl.multiple_of(row * 8, 8), 8), :] for p in range(lane_parts)],
                axis=1).astype(jnp.bfloat16)
            block = row * per_row + part
            terms[pl.ds(pl.multiple_of(block * 8, 8), 8), :] = jnp.dot(
                surface, regrid_v[block], preferred_element_type=jnp.float32)
        return carry

    lax.fori_loop(0, rows, regrid_row, 0)
    slots = count * NI
    select = (lax.broadcasted_iota(jnp.int32, (slots, blocks), 0) == target_ref[...])
    select = select.astype(jnp.float32).astype(jnp.bfloat16)
    for kind in range(species):
        value = terms[pl.ds(kind, blocks, stride=8), :]
        high = value.astype(jnp.bfloat16)
        rest = value - high.astype(jnp.float32)
        middle = rest.astype(jnp.bfloat16)
        low = (rest - middle.astype(jnp.float32)).astype(jnp.bfloat16)
        total = sum(
            jnp.dot(select, piece, preferred_element_type=jnp.float32) for piece in (high, middle, low))
        part_ref[:, kind] = total.reshape(count, NI, inv_cells)
    for level in range(levels):
        out_copy(level).wait()


def reduce_kernel(faces, tiles, part_ref, grad_ref, in_a, sum_a, in_b, sum_b, in_c,
                  send_a, recv_a, send_b, recv_b, send_c, recv_c):
    chips = tiles // 2
    face, tile = lax.axis_index("face"), lax.axis_index("tile")
    chip, core = tile // 2, lax.rem(tile, 2)
    partner = (face, tile + 1 - 2 * core)
    chip_of = [lax.rem(chip + step, chips) for step in range(chips)]
    face_of = [lax.rem(face + step, faces) for step in range(faces)]
    others = [partner]
    others += [(face, 2 * chip_of[step] + core) for step in range(1, chips)]
    others += [(face_of[step], tile) for step in range(1, faces)]
    barrier = pltpu.get_barrier_semaphore()
    for other in others:
        pl.semaphore_signal(barrier, inc=1, device_id=other, device_id_type=MESH)
    pl.semaphore_wait(barrier, len(others))

    order = list(range(1, chips)) + [0]
    first = {}
    for step in order:
        first[step] = pltpu.make_async_remote_copy(
            src_ref=part_ref.at[1 - core, chip_of[step]], dst_ref=in_a.at[step],
            send_sem=send_a.at[step], recv_sem=recv_a.at[step],
            device_id=partner, device_id_type=MESH)
        first[step].start()
    second = {}
    for step in order:
        first[step].wait_recv()
        sum_a[step] = part_ref[core, chip_of[step]] + in_a[step]
        if step > 0:
            second[step] = pltpu.make_async_remote_copy(
                src_ref=sum_a.at[step], dst_ref=in_b.at[step - 1],
                send_sem=send_b.at[step - 1], recv_sem=recv_b.at[step - 1],
                device_id=(face, 2 * chip_of[step] + core), device_id_type=MESH)
            second[step].start()
    for step in range(1, chips):
        second[step].wait_recv()
    total = sum_a[0]
    for step in range(1, chips):
        total = total + in_b[step - 1]
    sum_b[...] = total
    third = {}
    for step in range(1, faces):
        third[step] = pltpu.make_async_remote_copy(
            src_ref=sum_b.at[face_of[step]], dst_ref=in_c.at[step - 1],
            send_sem=send_c.at[step - 1], recv_sem=recv_c.at[step - 1],
            device_id=(face_of[step], tile), device_id_type=MESH)
        third[step].start()
    for step in range(1, faces):
        third[step].wait_recv()
    result = sum_b[face]
    for step in range(1, faces):
        result = result + in_c[step - 1]
    for kind in range(result.shape[0]):
        grad_ref[:, kind, :] = result[kind]
    for copies in (first, second, third):
        for copy in copies.values():
            copy.wait_send()


def per_device(faces, tiles, sensitivity, west_weight, east_weight, south_weight, north_weight,
               mixing_rate, extents, rotation, regrid_weight, owner, inv_slot):
    levels, species, rows, width = sensitivity.shape
    blocks, cells, inv_cells = regrid_weight.shape
    count, chips = faces * tiles, tiles // 2
    f32 = jnp.float32
    hbm = pl.BlockSpec(memory_space=pl.ANY)
    vmem = pl.BlockSpec(memory_space=pltpu.VMEM)
    smem = pl.BlockSpec(memory_space=pltpu.SMEM)
    dma = pltpu.SemaphoreType.DMA
    edge = jax.ShapeDtypeStruct((levels * species, width), f32)
    from_west, from_east = pl.pallas_call(
        functools.partial(edge_kernel, faces, tiles),
        out_shape=(edge, edge),
        in_specs=[smem, hbm, hbm, hbm],
        out_specs=(vmem, vmem),
        scratch_shapes=[
            pltpu.VMEM(sensitivity.shape, f32),
            pltpu.VMEM(west_weight.shape, f32),
            pltpu.VMEM(west_weight.shape, f32),
            pltpu.VMEM(edge.shape, f32),
            pltpu.VMEM(edge.shape, f32),
            dma((3,)), dma((2,)), dma((2,)),
        ],
        compiler_params=pltpu.CompilerParams(
            collective_id=0, has_side_effects=True, vmem_limit_bytes=60 << 20),
        name="edges",
    )(extents, sensitivity, west_weight, east_weight)

    owner_ids = owner[:, 0]
    owner_tile = owner_ids % tiles
    target = ((owner_tile % 2 * chips + owner_tile // 2) * faces + owner_ids // tiles) * NI + inv_slot
    adjoint_start, part = pl.pallas_call(
        functools.partial(tile_kernel, faces, tiles),
        out_shape=(
            jax.ShapeDtypeStruct(sensitivity.shape, f32),
            jax.ShapeDtypeStruct((count, species, NI, inv_cells), f32),
        ),
        in_specs=[smem, smem] + [hbm] * 9 + [vmem],
        out_specs=(hbm, vmem),
        scratch_shapes=[
            pltpu.VMEM(sensitivity.shape, f32),
            pltpu.VMEM(west_weight.shape, f32),
            pltpu.VMEM(west_weight.shape, f32),
            pltpu.VMEM(west_weight.shape, f32),
            pltpu.VMEM(west_weight.shape, f32),
            pltpu.VMEM((levels + 1, rows, width), f32),
            pltpu.VMEM(regrid_weight.shape, regrid_weight.dtype),
            pltpu.VMEM(edge.shape, f32),
            pltpu.VMEM(edge.shape, f32),
            pltpu.VMEM((levels, species, width), f32),
            pltpu.VMEM((levels, species, width), f32),
            pltpu.VMEM((levels + 1, species, rows, width), f32),
            pltpu.VMEM((levels + 1, rows, width), f32),
            pltpu.VMEM((width // LANES, rows * 8, LANES), f32),
            pltpu.VMEM((blocks * 8, inv_cells), f32),
            dma((5, levels)), dma, dma, dma((2,)), dma((levels,)),
        ],
        compiler_params=pltpu.CompilerParams(vmem_limit_bytes=60 << 20),
        name="tile",
    )(extents, rotation, sensitivity, west_weight, east_weight, south_weight, north_weight,
      mixing_rate, regrid_weight, from_west, from_east, target[None, :])

    unit = (species, NI, inv_cells)
    grad = pl.pallas_call(
        functools.partial(reduce_kernel, faces, tiles),
        out_shape=jax.ShapeDtypeStruct((NI, species, inv_cells), f32),
        in_specs=[vmem],
        out_specs=vmem,
        scratch_shapes=[
            pltpu.VMEM((chips, faces) + unit, f32),
            pltpu.VMEM((chips, faces) + unit, f32),
            pltpu.VMEM((chips - 1, faces) + unit, f32),
            pltpu.VMEM((faces,) + unit, f32),
            pltpu.VMEM((faces - 1,) + unit, f32),
            dma((chips,)), dma((chips,)), dma((chips - 1,)), dma((chips - 1,)),
            dma((faces - 1,)), dma((faces - 1,)),
        ],
        compiler_params=pltpu.CompilerParams(
            collective_id=1, has_side_effects=True, vmem_limit_bytes=24 << 20),
        name="reduce",
    )(part.reshape((2, chips, faces) + unit))
    return adjoint_start, grad


def solution(mesh):
    faces, tiles = mesh.shape["face"], mesh.shape["tile"]
    both = ("face", "tile")
    placed = (P(None, None, both, None),) + (P(None, both, None),) * 5 + (P(), P()) + (
        P(both, None, None), P(both, None), P(both))
    return jax.shard_map(
        functools.partial(per_device, faces, tiles),
        mesh=mesh,
        in_specs=placed,
        out_specs=(P(None, None, both, None), P(both, None, None)),
        check_vma=False,
    )
```

time: 271 us -> 41.7 us (0.15)
  waiting for transfers between devices: 111 us -> 0 us
  local copies, waits for them, and re-layouts: 97.9 us -> 1.64 us
  Pallas kernels: 0 us -> 38 us
  other arithmetic: 27.5 us -> 1.21 us
  between operations: 16.3 us -> 0.66 us
  matrix products: 8.9 us -> 0 us
  starting transfers between devices: 6.86 us -> 0 us
    reduce_scatter x1 -> x0, waiting for transfers between devices: 111 us -> none  [per_device(): lax.psum_scatter(jnp.dot(select.T, flat_terms, precision=lax.Precision.HI...]
    pallas_call x0 -> x3, Pallas kernels: none -> 38 us  [the longest x1 14.1 us: per_device(): pl.pallas_call(functools.partial(edge_kernel, faces, tiles), out_shape=(e...]
    mul x14 -> x0, local copies, waits for them, and re-layouts: 19 us -> none  [the longest x7 10.8 us: vertical_solve(): solved.append((rhs[level] + rate[level - 1] * solved[-1]) / pivot)]
    slice x5 -> x0, local copies, waits for them, and re-layouts: 18.4 us -> none  [the longest x1 9.72 us: vertical_solve(): solved = [rhs[0] / pivot]]
    squeeze x9 -> x0, local copies, waits for them, and re-layouts: 14.3 us -> none  [the longest x7 11.8 us: vertical_solve(): solved.append((rhs[level] + rate[level - 1] * solved[-1]) / pivot)]
    div x8 -> x0, local copies, waits for them, and re-layouts: 11.5 us -> none  [the longest x7 9.93 us: vertical_solve(): solved.append((rhs[level] + rate[level - 1] * solved[-1]) / pivot)]
    unnamed x66 -> x3, local copies, waits for them, and re-layouts: 12.1 us -> 1.64 us
    rev x2 -> x0, local copies, waits for them, and re-layouts: 9.81 us -> none  [the longest x1 4.98 us: per_device(): from_west = jnp.where(my_rotation == 1, jnp.flip(from_west, -1), from_west)]
  transfers between devices with their start and end apart: 3 -> 0, of which waited for: 1 -> 0; matrix products, arithmetic and copies ran while one was open for 28% -> 0% of each run, Pallas kernels for 0% -> 0%
where the time goes in v1:
time: 41.7 us; the launch traced here: 41.5 us
  Pallas kernels  38 us (91%)
  local copies, waits for them, and re-layouts  1.64 us (4%)
  other arithmetic  1.21 us (3%)
  between operations  0.66 us (2%)
    pallas_call x1, Pallas kernels, per_device(): pl.pallas_call(functools.partial(edge_kernel, faces, tiles), out_shape=(e...  14.1 us
    pallas_call x1, Pallas kernels, per_device(): pl.pallas_call(functools.partial(tile_kernel, faces, tiles), out_shape=(j...  13.1 us
    pallas_call x1, Pallas kernels, per_device(): pl.pallas_call(functools.partial(reduce_kernel, faces, tiles), out_shape=...  10.8 us
    unnamed x3, local copies, waits for them, and re-layouts  1.64 us
    broadcast_in_dim x1, other arithmetic, per_device(): target[None, :]  1.21 us

profile of v1, /device:TPU:0, one launch (start us, length us, event | category | flops | bytes accessed | tf_op | source)
XLA Modules:
  0.0 41.5 jit_solution(15684246670549346211)
XLA Ops:
  0.6 1.2 %add_bitcast_fusion.target_ref = s32[1,96]{1,0:T(1,128)} fusion(s32[96]{0:T(128)} %param.21, s32[96,1]{0,1:T(1,128)} %param.20), kind=kLoop, calls=%fused_computation.13 | loop fusion | flops 4224 | bytes 1152 | tf_op jit(solution)/shard_map/broadcast_in_dim | solution.py:356
  1.8 14.1 %edges.1 = (f32[32,1536]{1,0:T(8,128)}, f32[32,1536]{1,0:T(8,128)}) custom-call(s32[4,8]{1,0:T(4,128)} %ext_ref.3, f32[8,4,16,1536]{3,2,1,0:T(8,128)} %sens_hbm.3, f32[8,16,1536]{2,1,0:T(8,128)} %west_hbm.3, f32[8,16,1536]{2,1,0:T(8,128)} %east_hbm.3), custom_call_target="tpu_custom_call" | custom-call | tf_op jit(solution)/shard_map/edges/pallas_call | solution.py:306
  16.0 13.1 %tile.1 = (f32[8,4,16,1536]{3,2,1,0:T(8,128)}, f32[32,4,8,128]{3,2,1,0:T(8,128)}) custom-call(s32[4,8]{1,0:T(4,128)} %ext_ref.3, s32[4,8]{1,0:T(4,128)} %rot_ref.1, f32[8,4,16,1536]{3,2,1,0:T(8,128)} %sens_hbm.3, f32[8,16,1536]{2,1,0:T(8,128)} %west_hbm.3, f32[8,16,1536]{2,1,0:T(8,128)} %east_hbm.3, f32[8,16,1536]{2,1,0:T(8,128)} %south_hbm.1, ...), custom_call_target="tpu_custom_call" | custom-call | tf_op jit(solution)/shard_map/tile/pallas_call | solution.py:327
  29.0 0.0 copy-start
  29.1 1.0 %copy-done = f32[32,4,8,128]{3,2,1,0:T(8,128)S(1)} copy-done((f32[32,4,8,128]{3,2,1,0:T(8,128)S(1)}, f32[32,4,8,128]{3,2,1,0:T(8,128)}, u32[]{:S(2)}) %copy-start) | copy-done | bytes 524312
  30.1 10.8 %reduce.1 = f32[8,4,128]{2,1,0:T(4,128)S(1)} custom-call(f32[2,4,4,4,8,128]{5,4,3,2,1,0:T(8,128)S(1)} %bitcast.16), custom_call_target="tpu_custom_call" | custom-call | tf_op jit(solution)/shard_map/reduce/pallas_call | solution.py:359
  40.9 0.6 %copy.14 = f32[8,4,128]{2,1,0:T(4,128)} copy(f32[8,4,128]{2,1,0:T(4,128)S(1)} %reduce.1) | data formatting | bytes 32768
Async XLA Ops:
  29.0 1.0 %copy-start = (f32[32,4,8,128]{3,2,1,0:T(8,128)S(1)}, f32[32,4,8,128]{3,2,1,0:T(8,128)}, u32[]{:S(2)}) copy-start(f32[32,4,8,128]{3,2,1,0:T(8,128)} %get-tuple-element.9) | copy-start | bytes 1572868

commit v2 on v1

v2 whole, which is shorter than its diff:
```python
import functools

import jax
import jax.numpy as jnp
from jax import lax
from jax.experimental import pallas as pl
from jax.experimental.pallas import tpu as pltpu
from jax.sharding import PartitionSpec as P

NI = 8
LANES = 128
MESH = pl.DeviceIdType.MESH


def step_kernel(faces, tiles, ext_ref, rot_ref, sens_hbm, west_hbm, east_hbm, south_hbm, north_hbm,
                rate_hbm, regrid_hbm, owner_ref, slot_ref, solved, grad_ref,
                sens_v, west_v, east_v, south_v, north_v, rate_v, regrid_v, upper,
                east_edge, west_edge, from_west, from_east, edge, edge_south, edge_north, edge_rate, edge_upper,
                flat, terms, part_ref, in_a, sum_a, in_b, sum_b, in_c,
                level_sem, rate_sem, regrid_sem, edge_send, edge_recv,
                send_a, recv_a, send_b, recv_b, send_c, recv_c):
    levels, species, rows, width = sens_v.shape
    chunks = width // LANES
    blocks, cells, inv_cells = regrid_v.shape
    per_row = width // cells
    face, tile = lax.axis_index("face"), lax.axis_index("tile")
    count, chips = faces * tiles, tiles // 2
    position = face * tiles + tile
    after, before = lax.rem(position + 1, count), lax.rem(position + count - 1, count)
    after = (after // tiles, lax.rem(after, tiles))
    before = (before // tiles, lax.rem(before, tiles))
    chip, core = tile // 2, lax.rem(tile, 2)
    partner = (face, tile + 1 - 2 * core)
    chip_of = [lax.rem(chip + step, chips) for step in range(chips)]
    face_of = [lax.rem(face + step, faces) for step in range(faces)]
    others = [after, before, partner]
    others += [(face, 2 * chip_of[step] + core) for step in range(1, chips)]
    others += [(face_of[step], tile) for step in range(1, faces)]
    barrier = pltpu.get_barrier_semaphore()
    for other in others:
        pl.semaphore_signal(barrier, inc=1, device_id=other, device_id_type=MESH)

    def level_copies(level, pairs, base):
        return [
            pltpu.make_async_copy(source.at[level], sink.at[level], level_sem.at[base + number, level])
            for number, (source, sink) in enumerate(pairs)
        ]

    x_pairs = ((sens_hbm, sens_v), (west_hbm, west_v), (east_hbm, east_v))
    y_pairs = ((south_hbm, south_v), (north_hbm, north_v))
    rates = pltpu.make_async_copy(rate_hbm, rate_v.at[pl.ds(1, levels - 1)], rate_sem)
    regrid = pltpu.make_async_copy(regrid_hbm, regrid_v, regrid_sem)
    for level in range(levels):
        for copy in level_copies(level, x_pairs, 0):
            copy.start()
    rates.start()
    for level in range(levels):
        for copy in level_copies(level, y_pairs, 3):
            copy.start()
    regrid.start()

    extent = ext_ref[face, tile]
    row_ids = lax.broadcasted_iota(jnp.int32, (rows, LANES), 0)
    lane_ids = lax.broadcasted_iota(jnp.int32, (rows, LANES), 1)
    live = row_ids < extent
    first, last = row_ids == 0, row_ids == extent - 1
    bottom = row_ids == rows - 1
    lane_first, lane_last = lane_ids == 0, lane_ids == LANES - 1
    zero = jnp.zeros((rows, LANES), jnp.float32)
    zero_field = jnp.zeros((rows, width), jnp.float32)
    upper[0] = zero_field
    rate_v[0] = zero_field
    rate_v[levels] = zero_field
    for kind in range(species):
        solved[0, kind] = zero_field
    flat[...] = jnp.zeros_like(flat)

    def column(c):
        return slice(c * LANES, (c + 1) * LANES)

    for level in range(levels):
        for copy in level_copies(level, x_pairs, 0):
            copy.wait()
        for c in range(chunks):
            east_rows = jnp.where(last, east_v[level, :, column(c)], 0.0)
            for kind in range(species):
                row = level * species + kind
                east_edge[row:row + 1, column(c)] = jnp.sum(
                    east_rows * sens_v[level, kind, :, column(c)], axis=0, keepdims=True)
        west_row = west_v[level, 0:1, :]
        for kind in range(species):
            row = level * species + kind
            west_edge[row:row + 1, :] = west_row * sens_v[level, kind, 0:1, :]
    pl.semaphore_wait(barrier, len(others))
    exchange = [
        pltpu.make_async_remote_copy(
            src_ref=source, dst_ref=sink, send_sem=edge_send.at[number], recv_sem=edge_recv.at[number],
            device_id=other, device_id_type=MESH)
        for number, (source, sink, other) in enumerate(
            ((east_edge, from_west, after), (west_edge, from_east, before)))
    ]
    for copy in exchange:
        copy.start()

    rates.wait()
    half = lax.broadcasted_iota(jnp.int32, (8, LANES), 0) < species

    def edge_rows(value):
        tail = jnp.sum(jnp.where(last, value, 0.0), axis=0, keepdims=True)
        return jnp.where(half, jnp.broadcast_to(value[0:1], (8, LANES)), jnp.broadcast_to(tail, (8, LANES)))

    def forward(level, carry):
        for copy in level_copies(level, y_pairs, 3):
            copy.wait()
        previous = jnp.maximum(level - 1, 0)
        held = None
        behind = [zero] * species
        for c in range(chunks + 1):
            fresh = [(None, zero, zero)] * species
            if c < chunks:
                cols = column(c)
                west, east = west_v[level, :, cols], east_v[level, :, cols]
                south, north = south_v[level, :, cols], north_v[level, :, cols]
                edge_south[level, :, cols] = edge_rows(south)
                edge_north[level, :, cols] = edge_rows(north)
                keep_x = 1.0 - west - east
                keep_y = 1.0 - south - north
                fresh = []
                for kind in range(species):
                    adjoint = jnp.where(live, sens_v[level, kind, :, cols], 0.0)
                    up = jnp.where(bottom, 0.0, pltpu.roll(west * adjoint, rows - 1, 0))
                    down = jnp.where(first, 0.0, pltpu.roll(east * adjoint, 1, 0))
                    moved = jnp.where(live, keep_x * adjoint + up + down, 0.0)
                    fresh.append((
                        keep_y * moved,
                        pltpu.roll(south * moved, LANES - 1, 1),
                        pltpu.roll(north * moved, 1, 1),
                    ))
            if c > 0:
                cols = column(c - 1)
                low, high = rate_v[level, :, cols], rate_v[level + 1, :, cols]
                edge_rate[level + 1, :, cols] = edge_rows(high)
                pivot = (1.0 + low + high) + low * upper[level, :, cols]
                inverse = 1.0 / pivot
                upper[level + 1, :, cols] = -high * inverse
                for kind in range(species):
                    centre, left, right = held[kind]
                    y_adjoint = (centre + jnp.where(lane_last, fresh[kind][1], left)
                                 + jnp.where(lane_first, behind[kind], right))
                    solved[level, kind, :, cols] = (
                        y_adjoint + low * solved[previous, kind, :, cols]) * inverse
                behind = [held[kind][2] for kind in range(species)]
            held = fresh
        return carry

    lax.fori_loop(0, levels, forward, 0)

    after_rotation = rot_ref[after[0], after[1]]
    my_rotation = rot_ref[face, tile]
    back = (lax.broadcasted_iota(jnp.int32, (LANES, LANES), 0)
            + lax.broadcasted_iota(jnp.int32, (LANES, LANES), 1) == LANES - 1)
    back = back.astype(jnp.float32).astype(jnp.bfloat16)

    def pieces(value):
        high = value.astype(jnp.bfloat16)
        rest = value - high.astype(jnp.float32)
        middle = rest.astype(jnp.bfloat16)
        return high, middle, (rest - middle.astype(jnp.float32)).astype(jnp.bfloat16)

    for number, (source, rotation) in enumerate(((from_west, my_rotation), (from_east, after_rotation))):
        exchange[number].wait_recv()
        straight = jnp.concatenate([source[:, column(c)] for c in range(chunks)], axis=0)
        turned = sum(jnp.dot(piece, back, preferred_element_type=jnp.float32) for piece in pieces(straight))
        height = levels * species
        reverse = jnp.full((height, LANES), rotation, jnp.int32) == 1
        for c in range(chunks):
            mirrored = chunks - 1 - c
            value = jnp.where(reverse, turned[mirrored * height:(mirrored + 1) * height],
                              straight[c * height:(c + 1) * height])
            for level in range(levels):
                edge[level, number * species:(number + 1) * species, column(c)] = (
                    value[level * species:(level + 1) * species])

    zero_edge = jnp.zeros((8, width), jnp.float32)
    edge_rate[0] = zero_edge
    edge_upper[...] = zero_edge
    nothing = jnp.zeros((8, LANES), jnp.float32)

    def forward_edge(level, carry):
        previous = jnp.maximum(level - 1, 0)
        held, behind = None, nothing
        for c in range(chunks + 1):
            fresh = (None, nothing, nothing)
            if c < chunks:
                cols = column(c)
                south, north = edge_south[level, :, cols], edge_north[level, :, cols]
                moved = edge[level, :, cols]
                fresh = ((1.0 - south - north) * moved,
                         pltpu.roll(south * moved, LANES - 1, 1), pltpu.roll(north * moved, 1, 1))
            if c > 0:
                cols = column(c - 1)
                low, high = edge_rate[level, :, cols], edge_rate[level + 1, :, cols]
                inverse = 1.0 / ((1.0 + low + high) + low * edge_upper[:, cols])
                edge_upper[:, cols] = -high * inverse
                centre, left, right = held
                y_adjoint = (centre + jnp.where(lane_last[:8], fresh[1], left)
                             + jnp.where(lane_first[:8], behind, right))
                edge[level, :, cols] = (y_adjoint + low * edge[previous, :, cols]) * inverse
                behind = right
            held = fresh
        return carry

    lax.fori_loop(0, levels, forward_edge, 0)

    def backward(step, carry):
        level = levels - 1 - step
        later = jnp.minimum(level + 1, levels - 1)
        for c in range(chunks):
            cols = column(c)
            factor = upper[level + 1, :, cols]
            for kind in range(species):
                value = solved[level, kind, :, cols]
                value = value + jnp.where(first, edge[level, kind:kind + 1, cols], 0.0)
                value = value + jnp.where(last, edge[level, species + kind:species + kind + 1, cols], 0.0)
                solved[level, kind, :, cols] = value - factor * solved[later, kind, :, cols]
        return carry

    lax.fori_loop(0, levels, backward, 0)

    for c in range(chunks):
        for kind in range(species):
            flat[c, pl.ds(kind, rows, stride=8), :] = solved[0, kind, :, column(c)]
    regrid.wait()
    lane_parts = cells // LANES

    def regrid_row(row, carry):
        for part in range(per_row):
            surface = jnp.concatenate(
                [flat[part * lane_parts + p, pl.ds(pl.multiple_of(row * 8, 8), 8), :] for p in range(lane_parts)],
                axis=1).astype(jnp.bfloat16)
            block = row * per_row + part
            terms[pl.ds(pl.multiple_of(block * 8, 8), 8), :] = jnp.dot(
                surface, regrid_v[block], preferred_element_type=jnp.float32)
        return carry

    lax.fori_loop(0, rows, regrid_row, 0)
    target = owner_ref[...] * NI + slot_ref[...]
    select = lax.broadcasted_iota(jnp.int32, (count * NI, blocks), 0) == target
    select = select.astype(jnp.float32).astype(jnp.bfloat16)
    for kind in range(species):
        value = terms[pl.ds(kind, blocks, stride=8), :]
        total = sum(jnp.dot(select, piece, preferred_element_type=jnp.float32) for piece in pieces(value))
        for number in range(count):
            spot = (number % tiles % 2, number % tiles // 2, number // tiles, kind)
            part_ref[spot] = total[number * NI:(number + 1) * NI]

    order = list(range(1, chips)) + [0]
    first = {}
    for step in order:
        first[step] = pltpu.make_async_remote_copy(
            src_ref=part_ref.at[1 - core, chip_of[step]], dst_ref=in_a.at[step],
            send_sem=send_a.at[step], recv_sem=recv_a.at[step],
            device_id=partner, device_id_type=MESH)
        first[step].start()
    second = {}
    for step in order:
        first[step].wait_recv()
        sum_a[step] = part_ref[core, chip_of[step]] + in_a[step]
        if step > 0:
            second[step] = pltpu.make_async_remote_copy(
                src_ref=sum_a.at[step], dst_ref=in_b.at[step - 1],
                send_sem=send_b.at[step - 1], recv_sem=recv_b.at[step - 1],
                device_id=(face, 2 * chip_of[step] + core), device_id_type=MESH)
            second[step].start()
    for step in range(1, chips):
        second[step].wait_recv()
    total = sum_a[0]
    for step in range(1, chips):
        total = total + in_b[step - 1]
    sum_b[...] = total
    third = {}
    for step in range(1, faces):
        third[step] = pltpu.make_async_remote_copy(
            src_ref=sum_b.at[face_of[step]], dst_ref=in_c.at[step - 1],
            send_sem=send_c.at[step - 1], recv_sem=recv_c.at[step - 1],
            device_id=(face_of[step], tile), device_id_type=MESH)
        third[step].start()
    for step in range(1, faces):
        third[step].wait_recv()
    result = sum_b[face]
    for step in range(1, faces):
        result = result + in_c[step - 1]
    for kind in range(result.shape[0]):
        grad_ref[:, kind, :] = result[kind]
    for copies in (first, second, third):
        for copy in copies.values():
            copy.wait_send()
    for copy in exchange:
        copy.wait_send()


def per_device(faces, tiles, sensitivity, west_weight, east_weight, south_weight, north_weight,
               mixing_rate, extents, rotation, regrid_weight, owner, inv_slot):
    levels, species, rows, width = sensitivity.shape
    blocks, cells, inv_cells = regrid_weight.shape
    chips = tiles // 2
    f32 = jnp.float32
    hbm = pl.BlockSpec(memory_space=pltpu.HBM)
    vmem = pl.BlockSpec(memory_space=pltpu.VMEM)
    smem = pl.BlockSpec(memory_space=pltpu.SMEM)
    dma = pltpu.SemaphoreType.DMA
    unit = (species, NI, inv_cells)
    field, line, edge = (levels, rows, width), (levels * species, width), (levels, 2 * species, width)
    shapes = [sensitivity.shape] + [field] * 4 + [(levels + 1, rows, width)]
    scratch = [pltpu.VMEM(shape, f32) for shape in shapes]
    scratch += [pltpu.VMEM(regrid_weight.shape, regrid_weight.dtype)]
    shapes = [(levels + 1, rows, width)] + [line] * 4 + [edge] * 3
    shapes += [(levels + 1, 2 * species, width), (2 * species, width)]
    shapes += [(width // LANES, rows * 8, LANES), (blocks * 8, inv_cells)]
    shapes += [(2, chips, faces) + unit, (chips, faces) + unit, (chips, faces) + unit]
    shapes += [(chips - 1, faces) + unit, (faces,) + unit, (faces - 1,) + unit]
    scratch += [pltpu.VMEM(shape, f32) for shape in shapes]
    scratch += [dma((5, levels)), dma, dma, dma((2,)), dma((2,))]
    scratch += [dma((number,)) for number in (chips, chips, chips - 1, chips - 1, faces - 1, faces - 1)]
    return pl.pallas_call(
        functools.partial(step_kernel, faces, tiles),
        out_shape=(
            jax.ShapeDtypeStruct(sensitivity.shape, f32),
            jax.ShapeDtypeStruct((NI, species, inv_cells), f32),
        ),
        in_specs=[smem, smem] + [hbm] * 7 + [vmem, vmem],
        out_specs=(vmem, vmem),
        scratch_shapes=scratch,
        compiler_params=pltpu.CompilerParams(
            collective_id=0, has_side_effects=True, vmem_limit_bytes=44 << 20),
        name="step",
    )(extents, rotation, sensitivity, west_weight, east_weight, south_weight, north_weight,
      mixing_rate, regrid_weight, owner.reshape(1, blocks), inv_slot.reshape(1, blocks))


def solution(mesh):
    faces, tiles = mesh.shape["face"], mesh.shape["tile"]
    both = ("face", "tile")
    placed = (P(None, None, both, None),) + (P(None, both, None),) * 5 + (P(), P()) + (
        P(both, None, None), P(both, None), P(both))
    return jax.shard_map(
        functools.partial(per_device, faces, tiles),
        mesh=mesh,
        in_specs=placed,
        out_specs=(P(None, None, both, None), P(both, None, None)),
        check_vma=False,
    )
```

time: 41.7 us -> 46.3 us (1.11)
  local copies, waits for them, and re-layouts: 1.64 us -> 12.5 us
  Pallas kernels: 38 us -> 32.7 us
  other arithmetic: 1.21 us -> 0 us
    unnamed x3 -> x22, local copies, waits for them, and re-layouts: 1.64 us -> 12.5 us
    pallas_call x3 -> x1, Pallas kernels: 38 us -> 32.7 us  [per_device(): pl.pallas_call(functools.partial(step_kernel, faces, tiles), out_shape=(j...]
    broadcast_in_dim x1 -> x0, other arithmetic: 1.21 us -> none  [per_device(): target[None, :]]
where the time goes in v2:
time: 46.3 us; the launch traced here: 45.8 us
  Pallas kernels  32.7 us (71%)
  local copies, waits for them, and re-layouts  12.5 us (27%)
  between operations  0.66 us (1%)
    pallas_call x1, Pallas kernels, per_device(): pl.pallas_call(functools.partial(step_kernel, faces, tiles), out_shape=(j...  32.7 us
    unnamed x22, local copies, waits for them, and re-layouts  12.5 us

profile of v2, /device:TPU:0, one launch (start us, length us, event | category | flops | bytes accessed | tf_op | source)
XLA Modules:
  0.0 45.8 jit_solution(10602210395012007826)
XLA Ops:
  0.6 0.0 copy-start
  0.6 1.9 %copy-done = f32[8,4,16,1536]{3,2,1,0:T(8,128)S(1)} copy-done((f32[8,4,16,1536]{3,2,1,0:T(8,128)S(1)}, f32[8,4,16,1536]{3,2,1,0:T(8,128)}, u32[]{:S(2)}) %copy-start) | copy-done | bytes 3145752
  2.5 0.0 copy-start.1
  2.5 1.1 %copy-done.1 = f32[8,16,1536]{2,1,0:T(8,128)S(1)} copy-done((f32[8,16,1536]{2,1,0:T(8,128)S(1)}, f32[8,16,1536]{2,1,0:T(8,128)}, u32[]{:S(2)}) %copy-start.1) | copy-done | bytes 786456
  3.7 0.0 copy-start.2
  3.7 1.1 %copy-done.2 = f32[8,16,1536]{2,1,0:T(8,128)S(1)} copy-done((f32[8,16,1536]{2,1,0:T(8,128)S(1)}, f32[8,16,1536]{2,1,0:T(8,128)}, u32[]{:S(2)}) %copy-start.2) | copy-done | bytes 786456
  4.8 0.0 copy-start.3
  4.8 1.1 %copy-done.3 = f32[8,16,1536]{2,1,0:T(8,128)S(1)} copy-done((f32[8,16,1536]{2,1,0:T(8,128)S(1)}, f32[8,16,1536]{2,1,0:T(8,128)}, u32[]{:S(2)}) %copy-start.3) | copy-done | bytes 786456
  5.9 0.0 copy-start.4
  5.9 1.1 %copy-done.4 = f32[8,16,1536]{2,1,0:T(8,128)S(1)} copy-done((f32[8,16,1536]{2,1,0:T(8,128)S(1)}, f32[8,16,1536]{2,1,0:T(8,128)}, u32[]{:S(2)}) %copy-start.4) | copy-done | bytes 786456
  7.1 0.0 copy-start.5
  7.1 1.1 %copy-done.5 = f32[7,16,1536]{2,1,0:T(8,128)S(1)} copy-done((f32[7,16,1536]{2,1,0:T(8,128)S(1)}, f32[7,16,1536]{2,1,0:T(8,128)}, u32[]{:S(2)}) %copy-start.5) | copy-done | bytes 688152
  8.2 0.0 copy-start.6
  8.2 0.7 %copy-done.6 = s32[4,8]{1,0:T(4,128)S(1)} copy-done((s32[4,8]{1,0:T(4,128)S(1)}, s32[4,8]{1,0:T(4,128)}, u32[]{:S(2)}) %copy-start.6) | copy-done | bytes 152
  8.8 0.0 copy-start.7
  8.8 0.7 %copy-done.7 = s32[4,8]{1,0:T(4,128)S(1)} copy-done((s32[4,8]{1,0:T(4,128)S(1)}, s32[4,8]{1,0:T(4,128)}, u32[]{:S(2)}) %copy-start.7) | copy-done | bytes 152
  9.5 0.0 copy-start.8
  9.5 0.7 %copy-done.8 = s32[96,1]{0,1:T(1,128)S(1)} copy-done((s32[96,1]{0,1:T(1,128)S(1)}, s32[96,1]{0,1:T(1,128)}, u32[]{:S(2)}) %copy-start.8) | copy-done | bytes 408
  10.2 0.0 copy-start.9
  10.2 0.7 %copy-done.9 = s32[96]{0:T(128)S(1)} copy-done((s32[96]{0:T(128)S(1)}, s32[96]{0:T(128)}, u32[]{:S(2)}) %copy-start.9) | copy-done | bytes 408
  10.8 32.7 %step.1 = (f32[8,4,16,1536]{3,2,1,0:T(8,128)S(1)}, f32[8,4,128]{2,1,0:T(4,128)S(1)}) custom-call(s32[4,8]{1,0:T(4,128)S(1)} %copy-done.6, s32[4,8]{1,0:T(4,128)S(1)} %copy-done.7, f32[8,4,16,1536]{3,2,1,0:T(8,128)S(1)} %copy-done, f32[8,16,1536]{2,1,0:T(8,128)S(1)} %copy-done.1, f32[8,16,1536]{2,1,0:T(8,128)S(1)} %copy-done.2, f32[8,16,1536]{2,1,0:T(8,128)S(1)} %copy-done.3, ...), custom_call_target="tpu_custom_call" | custom-call | tf_op jit(solution)/shard_map/step/pallas_call | solution.py:325
  43.6 1.7 %copy.15 = f32[8,4,16,1536]{3,2,1,0:T(8,128)} copy(f32[8,4,16,1536]{3,2,1,0:T(8,128)S(1)} %get-tuple-element.4) | data formatting | bytes 6291456
  45.2 0.6 %copy.16 = f32[8,4,128]{2,1,0:T(4,128)} copy(f32[8,4,128]{2,1,0:T(4,128)S(1)} %get-tuple-element.5) | data formatting | bytes 32768
Async XLA Ops:
  0.6 1.9 %copy-start = (f32[8,4,16,1536]{3,2,1,0:T(8,128)S(1)}, f32[8,4,16,1536]{3,2,1,0:T(8,128)}, u32[]{:S(2)}) copy-start(f32[8,4,16,1536]{3,2,1,0:T(8,128)} %sens_hbm.1) | copy-start | bytes 9437188
  2.5 1.1 %copy-start.1 = (f32[8,16,1536]{2,1,0:T(8,128)S(1)}, f32[8,16,1536]{2,1,0:T(8,128)}, u32[]{:S(2)}) copy-start(f32[8,16,1536]{2,1,0:T(8,128)} %west_hbm.1) | copy-start | bytes 2359300
  3.7 1.1 %copy-start.2 = (f32[8,16,1536]{2,1,0:T(8,128)S(1)}, f32[8,16,1536]{2,1,0:T(8,128)}, u32[]{:S(2)}) copy-start(f32[8,16,1536]{2,1,0:T(8,128)} %east_hbm.1) | copy-start | bytes 2359300
  4.8 1.1 %copy-start.3 = (f32[8,16,1536]{2,1,0:T(8,128)S(1)}, f32[8,16,1536]{2,1,0:T(8,128)}, u32[]{:S(2)}) copy-start(f32[8,16,1536]{2,1,0:T(8,128)} %south_hbm.1) | copy-start | bytes 2359300
  5.9 1.1 %copy-start.4 = (f32[8,16,1536]{2,1,0:T(8,128)S(1)}, f32[8,16,1536]{2,1,0:T(8,128)}, u32[]{:S(2)}) copy-start(f32[8,16,1536]{2,1,0:T(8,128)} %north_hbm.1) | copy-start | bytes 2359300
  7.1 1.1 %copy-start.5 = (f32[7,16,1536]{2,1,0:T(8,128)S(1)}, f32[7,16,1536]{2,1,0:T(8,128)}, u32[]{:S(2)}) copy-start(f32[7,16,1536]{2,1,0:T(8,128)} %rate_hbm.1) | copy-start | bytes 2064388
  8.2 0.7 %copy-start.6 = (s32[4,8]{1,0:T(4,128)S(1)}, s32[4,8]{1,0:T(4,128)}, u32[]{:S(2)}) copy-start(s32[4,8]{1,0:T(4,128)} %ext_ref.1) | copy-start | bytes 388
  8.8 0.7 %copy-start.7 = (s32[4,8]{1,0:T(4,128)S(1)}, s32[4,8]{1,0:T(4,128)}, u32[]{:S(2)}) copy-start(s32[4,8]{1,0:T(4,128)} %rot_ref.1) | copy-start | bytes 388
  9.5 0.7 %copy-start.8 = (s32[96,1]{0,1:T(1,128)S(1)}, s32[96,1]{0,1:T(1,128)}, u32[]{:S(2)}) copy-start(s32[96,1]{0,1:T(1,128)} %param.20) | copy-start | bytes 1156
  10.2 0.7 %copy-start.9 = (s32[96]{0:T(128)S(1)}, s32[96]{0:T(128)}, u32[]{:S(2)}) copy-start(s32[96]{0:T(128)} %param.21) | copy-start | bytes 1156

commit v3 on v2

--- a/solution.py
+++ b/solution.py
@@ -13,11 +13,11 @@
 
 
 def step_kernel(faces, tiles, ext_ref, rot_ref, sens_hbm, west_hbm, east_hbm, south_hbm, north_hbm,
-                rate_hbm, regrid_hbm, owner_ref, slot_ref, solved, grad_ref,
-                sens_v, west_v, east_v, south_v, north_v, rate_v, regrid_v, upper,
+                rate_hbm, regrid_hbm, owner_ref, slot_ref, out_hbm, grad_ref,
+                sens_v, west_v, east_v, south_v, north_v, rate_v, regrid_v, solved, upper,
                 east_edge, west_edge, from_west, from_east, edge, edge_south, edge_north, edge_rate, edge_upper,
                 flat, terms, part_ref, in_a, sum_a, in_b, sum_b, in_c,
-                level_sem, rate_sem, regrid_sem, edge_send, edge_recv,
+                level_sem, rate_sem, regrid_sem, edge_send, edge_recv, out_sem,
                 send_a, recv_a, send_b, recv_b, send_c, recv_c):
     levels, species, rows, width = sens_v.shape
     chunks = width // LANES
@@ -212,6 +212,9 @@
 
     lax.fori_loop(0, levels, forward_edge, 0)
 
+    def out_copy(level):
+        return pltpu.make_async_copy(solved.at[level], out_hbm.at[level], out_sem.at[level])
+
     def backward(step, carry):
         level = levels - 1 - step
         later = jnp.minimum(level + 1, levels - 1)
@@ -223,6 +226,7 @@
                 value = value + jnp.where(first, edge[level, kind:kind + 1, cols], 0.0)
                 value = value + jnp.where(last, edge[level, species + kind:species + kind + 1, cols], 0.0)
                 solved[level, kind, :, cols] = value - factor * solved[later, kind, :, cols]
+        out_copy(level).start()
         return carry
 
     lax.fori_loop(0, levels, backward, 0)
@@ -297,6 +301,8 @@
             copy.wait_send()
     for copy in exchange:
         copy.wait_send()
+    for level in range(levels):
+        out_copy(level).wait()
 
 
 def per_device(faces, tiles, sensitivity, west_weight, east_weight, south_weight, north_weight,
@@ -314,13 +320,13 @@
     shapes = [sensitivity.shape] + [field] * 4 + [(levels + 1, rows, width)]
     scratch = [pltpu.VMEM(shape, f32) for shape in shapes]
     scratch += [pltpu.VMEM(regrid_weight.shape, regrid_weight.dtype)]
-    shapes = [(levels + 1, rows, width)] + [line] * 4 + [edge] * 3
+    shapes = [sensitivity.shape, (levels + 1, rows, width)] + [line] * 4 + [edge] * 3
     shapes += [(levels + 1, 2 * species, width), (2 * species, width)]
     shapes += [(width // LANES, rows * 8, LANES), (blocks * 8, inv_cells)]
     shapes += [(2, chips, faces) + unit, (chips, faces) + unit, (chips, faces) + unit]
     shapes += [(chips - 1, faces) + unit, (faces,) + unit, (faces - 1,) + unit]
     scratch += [pltpu.VMEM(shape, f32) for shape in shapes]
-    scratch += [dma((5, levels)), dma, dma, dma((2,)), dma((2,))]
+    scratch += [dma((5, levels)), dma, dma, dma((2,)), dma((2,)), dma((levels,))]
     scratch += [dma((number,)) for number in (chips, chips, chips - 1, chips - 1, faces - 1, faces - 1)]
     return pl.pallas_call(
         functools.partial(step_kernel, faces, tiles),
@@ -329,10 +335,10 @@
             jax.ShapeDtypeStruct((NI, species, inv_cells), f32),
         ),
         in_specs=[smem, smem] + [hbm] * 7 + [vmem, vmem],
-        out_specs=(vmem, vmem),
+        out_specs=(hbm, vmem),
         scratch_shapes=scratch,
         compiler_params=pltpu.CompilerParams(
-            collective_id=0, has_side_effects=True, vmem_limit_bytes=44 << 20),
+            collective_id=0, has_side_effects=True, vmem_limit_bytes=60 << 20),
         name="step",
     )(extents, rotation, sensitivity, west_weight, east_weight, south_weight, north_weight,
       mixing_rate, regrid_weight, owner.reshape(1, blocks), inv_slot.reshape(1, blocks))

time: 46.3 us -> 34.8 us (0.75)
  local copies, waits for them, and re-layouts: 12.5 us -> 4.5 us
  Pallas kernels: 32.7 us -> 29.5 us
    unnamed x22 -> x4, local copies, waits for them, and re-layouts: 12.5 us -> 4.5 us
    pallas_call x1, Pallas kernels: 32.7 us -> 29.5 us  [per_device(): pl.pallas_call(functools.partial(step_kernel, faces, tiles), out_shape=(j...]
where the time goes in v3:
time: 34.8 us; the launch traced here: 34.7 us
  Pallas kernels  29.5 us (85%)
  local copies, waits for them, and re-layouts  4.5 us (13%)
  between operations  0.65 us (2%)
    pallas_call x1, Pallas kernels, per_device(): pl.pallas_call(functools.partial(step_kernel, faces, tiles), out_shape=(j...  29.5 us
    unnamed x4, local copies, waits for them, and re-layouts  4.5 us

profile of v3, /device:TPU:0, one launch (start us, length us, event | category | flops | bytes accessed | tf_op | source)
XLA Modules:
  0.0 34.7 jit_solution(1884930853059441998)
XLA Ops:
  0.6 29.5 %step.1 = (f32[8,4,16,1536]{3,2,1,0:T(8,128)}, f32[8,4,128]{2,1,0:T(4,128)}) custom-call(s32[4,8]{1,0:T(4,128)} %ext_ref.1, s32[4,8]{1,0:T(4,128)} %rot_ref.1, f32[8,4,16,1536]{3,2,1,0:T(8,128)} %sens_hbm.1, f32[8,16,1536]{2,1,0:T(8,128)} %west_hbm.1, f32[8,16,1536]{2,1,0:T(8,128)} %east_hbm.1, f32[8,16,1536]{2,1,0:T(8,128)} %south_hbm.1, ...), custom_call_target="tpu_custom_call" | custom-call | tf_op jit(solution)/shard_map/step/pallas_call | solution.py:331
  30.2 0.0 copy-start
  30.2 3.9 %copy.15 = f32[8,4,16,1536]{3,2,1,0:T(8,128)} copy(f32[8,4,16,1536]{3,2,1,0:T(8,128)} %get-tuple-element.4) | data formatting | bytes 6291456
  34.1 0.0 copy-done
  34.1 0.6 %copy.16 = f32[8,4,128]{2,1,0:T(4,128)} copy(f32[8,4,128]{2,1,0:T(4,128)S(1)} %copy-done) | data formatting | bytes 32768
Async XLA Ops:
  30.2 3.9 %copy-start = (f32[8,4,128]{2,1,0:T(4,128)S(1)}, f32[8,4,128]{2,1,0:T(4,128)}, u32[]{:S(2)}) copy-start(f32[8,4,128]{2,1,0:T(4,128)} %get-tuple-element.5) | copy-start | bytes 49156

commit v4 on v2

--- a/solution.py
+++ b/solution.py
@@ -12,12 +12,12 @@
 MESH = pl.DeviceIdType.MESH
 
 
-def step_kernel(faces, tiles, ext_ref, rot_ref, sens_hbm, west_hbm, east_hbm, south_hbm, north_hbm,
-                rate_hbm, regrid_hbm, owner_ref, slot_ref, solved, grad_ref,
+def step_kernel(faces, tiles, ext_hbm, rot_hbm, sens_hbm, west_hbm, east_hbm, south_hbm, north_hbm,
+                rate_hbm, regrid_hbm, owner_hbm, slot_hbm, solved, grad_ref,
                 sens_v, west_v, east_v, south_v, north_v, rate_v, regrid_v, upper,
                 east_edge, west_edge, from_west, from_east, edge, edge_south, edge_north, edge_rate, edge_upper,
                 flat, terms, part_ref, in_a, sum_a, in_b, sum_b, in_c,
-                level_sem, rate_sem, regrid_sem, edge_send, edge_recv,
+                ext_ref, rot_ref, owner_ref, slot_ref, small_sem, level_sem, rate_sem, regrid_sem, edge_send, edge_recv,
                 send_a, recv_a, send_b, recv_b, send_c, recv_c):
     levels, species, rows, width = sens_v.shape
     chunks = width // LANES
@@ -50,6 +50,13 @@
     y_pairs = ((south_hbm, south_v), (north_hbm, north_v))
     rates = pltpu.make_async_copy(rate_hbm, rate_v.at[pl.ds(1, levels - 1)], rate_sem)
     regrid = pltpu.make_async_copy(regrid_hbm, regrid_v, regrid_sem)
+    small = [
+        pltpu.make_async_copy(source, sink, small_sem.at[number])
+        for number, (source, sink) in enumerate(
+            ((ext_hbm, ext_ref), (rot_hbm, rot_ref), (owner_hbm, owner_ref), (slot_hbm, slot_ref)))
+    ]
+    for copy in small:
+        copy.start()
     for level in range(levels):
         for copy in level_copies(level, x_pairs, 0):
             copy.start()
@@ -59,6 +66,8 @@
             copy.start()
     regrid.start()
 
+    for copy in small:
+        copy.wait()
     extent = ext_ref[face, tile]
     row_ids = lax.broadcasted_iota(jnp.int32, (rows, LANES), 0)
     lane_ids = lax.broadcasted_iota(jnp.int32, (rows, LANES), 1)
@@ -247,25 +256,26 @@
     target = owner_ref[...] * NI + slot_ref[...]
     select = lax.broadcasted_iota(jnp.int32, (count * NI, blocks), 0) == target
     select = select.astype(jnp.float32).astype(jnp.bfloat16)
+    first = {}
     for kind in range(species):
         value = terms[pl.ds(kind, blocks, stride=8), :]
         total = sum(jnp.dot(select, piece, preferred_element_type=jnp.float32) for piece in pieces(value))
         for number in range(count):
-            spot = (number % tiles % 2, number % tiles // 2, number // tiles, kind)
+            spot = (number % tiles % 2, kind, number % tiles // 2, number // tiles)
             part_ref[spot] = total[number * NI:(number + 1) * NI]
+        first[kind] = pltpu.make_async_remote_copy(
+            src_ref=part_ref.at[1 - core, kind], dst_ref=in_a.at[kind],
+            send_sem=send_a.at[kind], recv_sem=recv_a.at[kind],
+            device_id=partner, device_id_type=MESH)
+        first[kind].start()
 
     order = list(range(1, chips)) + [0]
-    first = {}
-    for step in order:
-        first[step] = pltpu.make_async_remote_copy(
-            src_ref=part_ref.at[1 - core, chip_of[step]], dst_ref=in_a.at[step],
-            send_sem=send_a.at[step], recv_sem=recv_a.at[step],
-            device_id=partner, device_id_type=MESH)
-        first[step].start()
+    for kind in range(species):
+        first[kind].wait_recv()
     second = {}
     for step in order:
-        first[step].wait_recv()
-        sum_a[step] = part_ref[core, chip_of[step]] + in_a[step]
+        for kind in range(species):
+            sum_a[step, :, kind] = part_ref[core, kind, chip_of[step]] + in_a[kind, chip_of[step]]
         if step > 0:
             second[step] = pltpu.make_async_remote_copy(
                 src_ref=sum_a.at[step], dst_ref=in_b.at[step - 1],
@@ -307,7 +317,6 @@
     f32 = jnp.float32
     hbm = pl.BlockSpec(memory_space=pltpu.HBM)
     vmem = pl.BlockSpec(memory_space=pltpu.VMEM)
-    smem = pl.BlockSpec(memory_space=pltpu.SMEM)
     dma = pltpu.SemaphoreType.DMA
     unit = (species, NI, inv_cells)
     field, line, edge = (levels, rows, width), (levels * species, width), (levels, 2 * species, width)
@@ -317,25 +326,29 @@
     shapes = [(levels + 1, rows, width)] + [line] * 4 + [edge] * 3
     shapes += [(levels + 1, 2 * species, width), (2 * species, width)]
     shapes += [(width // LANES, rows * 8, LANES), (blocks * 8, inv_cells)]
-    shapes += [(2, chips, faces) + unit, (chips, faces) + unit, (chips, faces) + unit]
+    tail = (chips, faces, NI, inv_cells)
+    shapes += [(2, species) + tail, (species,) + tail, (chips, faces) + unit]
     shapes += [(chips - 1, faces) + unit, (faces,) + unit, (faces - 1,) + unit]
     scratch += [pltpu.VMEM(shape, f32) for shape in shapes]
-    scratch += [dma((5, levels)), dma, dma, dma((2,)), dma((2,))]
-    scratch += [dma((number,)) for number in (chips, chips, chips - 1, chips - 1, faces - 1, faces - 1)]
+    scratch += [pltpu.SMEM(extents.shape, jnp.int32)] * 2 + [pltpu.VMEM((1, blocks), jnp.int32)] * 2
+    scratch += [dma((4,)), dma((5, levels)), dma, dma, dma((2,)), dma((2,))]
+    scratch += [dma((number,)) for number in (species, species, chips - 1, chips - 1, faces - 1, faces - 1)]
+    pin = functools.partial(pltpu.with_memory_space_constraint, memory_space=pltpu.HBM)
+    operands = (extents, rotation, sensitivity, west_weight, east_weight, south_weight, north_weight,
+                mixing_rate, regrid_weight, owner.reshape(1, blocks), inv_slot.reshape(1, blocks))
     return pl.pallas_call(
         functools.partial(step_kernel, faces, tiles),
         out_shape=(
             jax.ShapeDtypeStruct(sensitivity.shape, f32),
             jax.ShapeDtypeStruct((NI, species, inv_cells), f32),
         ),
-        in_specs=[smem, smem] + [hbm] * 7 + [vmem, vmem],
+        in_specs=[hbm] * 11,
         out_specs=(vmem, vmem),
         scratch_shapes=scratch,
         compiler_params=pltpu.CompilerParams(
             collective_id=0, has_side_effects=True, vmem_limit_bytes=44 << 20),
         name="step",
-    )(extents, rotation, sensitivity, west_weight, east_weight, south_weight, north_weight,
-      mixing_rate, regrid_weight, owner.reshape(1, blocks), inv_slot.reshape(1, blocks))
+    )(*[pin(operand) for operand in operands])
 
 
 def solution(mesh):

time: 46.3 us -> 32.6 us (0.70)
  local copies, waits for them, and re-layouts: 12.5 us -> 2.27 us
  Pallas kernels: 32.7 us -> 29.5 us
    unnamed x22 -> x2, local copies, waits for them, and re-layouts: 12.5 us -> 2.27 us
    pallas_call x1, Pallas kernels: 32.7 us -> 29.5 us  [per_device(): pl.pallas_call(functools.partial(step_kernel, faces, tiles), out_shape=(j...]
where the time goes in v4:
time: 32.6 us; the launch traced here: 32.5 us
  Pallas kernels  29.5 us (90%)
  local copies, waits for them, and re-layouts  2.27 us (7%)
  between operations  0.64 us (2%)
    pallas_call x1, Pallas kernels, per_device(): pl.pallas_call(functools.partial(step_kernel, faces, tiles), out_shape=(j...  29.5 us
    unnamed x2, local copies, waits for them, and re-layouts  2.27 us

profile of v4, /device:TPU:0, one launch (start us, length us, event | category | flops | bytes accessed | tf_op | source)
XLA Modules:
  0.0 32.5 jit_solution(2986695997110007773)
XLA Ops:
  0.6 29.5 %step.1 = (f32[8,4,16,1536]{3,2,1,0:T(8,128)S(1)}, f32[8,4,128]{2,1,0:T(4,128)S(1)}) custom-call(s32[4,8]{1,0:T(4,128)} %ext_hbm.1, s32[4,8]{1,0:T(4,128)} %rot_hbm.1, f32[8,4,16,1536]{3,2,1,0:T(8,128)} %sens_hbm.1, f32[8,16,1536]{2,1,0:T(8,128)} %west_hbm.1, f32[8,16,1536]{2,1,0:T(8,128)} %east_hbm.1, f32[8,16,1536]{2,1,0:T(8,128)} %south_hbm.1, ...), custom_call_target="tpu_custom_call" | custom-call | tf_op jit(solution)/shard_map/step/pallas_call | solution.py:339
  30.2 1.7 %copy.15 = f32[8,4,16,1536]{3,2,1,0:T(8,128)} copy(f32[8,4,16,1536]{3,2,1,0:T(8,128)S(1)} %get-tuple-element.4) | data formatting | bytes 6291456
  31.8 0.6 %copy.16 = f32[8,4,128]{2,1,0:T(4,128)} copy(f32[8,4,128]{2,1,0:T(4,128)S(1)} %get-tuple-element.5) | data formatting | bytes 32768
